TPU v7x, 256 devices: a whole 4x4x8 slice. The times are simulated.
256 devices in a mesh: row: 8 (over y, core), col: 32 (over z, x).
Axes of the slice: x: 4, y: 4, z: 8, core: 2. Of those that a mesh axis runs over, the one named last changes fastest.
Arguments:
- params: float32 [64, 8192], replicated, may hold values from -6 to 6
- momentum: float32 [8, 32, 64, 8192], P('row', 'col'), may hold values from -6 to 6
- gradient: float32 [8, 32, 64, 8192], P('row', 'col'), may hold values from -6 to 6
- chosen_rows: int32 [8, 32, 128, 4], P('row', 'col'), may hold values from 0 to 63, as said below
- live_counts: int32 [8, 32, 128], P('row', 'col'), may hold values from 1 to 4, as said below
- common_rows: int32 [32, 128, 8], P('col'), may hold values from 0 to 63, as said below
Outputs:
- new_params: float32 [64, 8192], replicated
- new_momentum: float32 [8, 32, 64, 8192], P('row', 'col')
Inputs may be any that keep to these rules, and one draw needn't show every extreme that they name: `chosen_rows`: within one replica's block the 4 entries are distinct; entries at positions at or past the block's live count are ignored. `live_counts`: every replica has 4 live rows in some block. `common_rows`: within one group's block the 8 entries are distinct.
All inputs are finite; a program needn't handle non-finite values.
Results may differ from a plain program's by a relative error of at most 0.0003.
Values sent between devices are 32-bit elements; how exact they have to be, the bound alone decides.
A program may use at most 128 MiB of HBM per device.

v0:
```python
import math

import jax
import jax.numpy as jnp
from jax import lax
from jax.sharding import PartitionSpec as P

CH = 64


decay_rate = 0.9
step_size = 0.1
highest = lax.Precision.HIGHEST


def from_everyone(array, axis):
    devices = lax.axis_size(axis)
    return lax.all_to_all(
        jnp.broadcast_to(array[None], (devices, *array.shape)), axis, 0, 0, tiled=True
    )


def of_everyone(array, axis):
    everything = from_everyone(array, axis)
    return jnp.sum(everything, axis=0)


def dct_table(order):
    freq = jnp.arange(order, dtype=jnp.float32)[:, None]
    place = jnp.arange(order, dtype=jnp.float32)[None, :]
    matrix = math.sqrt(2.0 / order) * jnp.cos(math.pi * (2.0 * place + 1.0) * freq / (2.0 * order))
    return jnp.where(freq == 0.0, matrix * math.sqrt(0.5), matrix)


def block_pair(matrix):
    return jnp.kron(jnp.eye(2, dtype=jnp.float32), matrix)


def forward(field):
    matrix = dct_table(CH)
    across = jnp.dot(matrix, field, precision=highest, preferred_element_type=jnp.float32)
    shaped = across.reshape(-1, 2 * CH)
    result = jnp.dot(
        shaped, block_pair(matrix.T), precision=highest, preferred_element_type=jnp.float32
    )
    return result.reshape(field.shape)


def inverse(field):
    matrix = dct_table(CH)
    across = jnp.dot(matrix.T, field, precision=highest, preferred_element_type=jnp.float32)
    shaped = across.reshape(-1, 2 * CH)
    result = jnp.dot(
        shaped, block_pair(matrix), precision=highest, preferred_element_type=jnp.float32
    )
    return result.reshape(field.shape)


def pick_table(chosen, counts):
    table = (chosen[..., None] == jnp.arange(CH, dtype=jnp.int32)).astype(jnp.float32)
    if counts is not None:
        live = (jnp.arange(chosen.shape[-1], dtype=jnp.int32) < counts[..., None]).astype(
            jnp.float32
        )
        table = table * live[..., None]
    return table


def body(params, momentum, gradient, chosen_rows, live_counts, common_rows):
    decayed = decay_rate * momentum[0, 0] + gradient[0, 0]
    spectrum = forward(decayed)
    blocks = spectrum.shape[1] // CH
    cube = spectrum.reshape(CH, blocks, CH)
    picked = pick_table(chosen_rows[0, 0], live_counts[0, 0])
    values = jnp.einsum("ksf,fkg->ksg", picked, cube, precision=highest)
    sent = jnp.einsum("ksf,ksg->fkg", picked, values, precision=highest)
    residual = decayed - inverse(sent.reshape(CH, -1))
    cut_table = pick_table(common_rows[0], None)
    update = None
    matches = jnp.einsum("kqf,ksf->kqs", cut_table, picked, precision=highest)
    own_part = jnp.einsum("kqs,ksg->kqg", matches, values, precision=highest)
    kept = of_everyone(own_part, "row")
    vals = lax.all_gather(kept.reshape(1, blocks, -1), "col", axis=0, tiled=True)
    lists = lax.all_gather(common_rows, "col", axis=0, tiled=True)
    table = pick_table(lists, None)
    shaped = vals.reshape(vals.shape[0], blocks, -1, CH)
    total = jnp.einsum("nkqf,nkqg->fkg", table, shaped, precision=highest)
    update = inverse(total.reshape(CH, -1))
    new_params = params - step_size * update
    return (new_params, residual[None, None])


def solution(mesh):
    placed = (
        P(),
        P("row", "col", None, None),
        P("row", "col", None, None),
        P("row", "col", None, None),
        P("row", "col", None),
        P("col", None, None),
    )
    return jax.shard_map(
        body,
        mesh=mesh,
        in_specs=placed,
        out_specs=(P(), P("row", "col", None, None)),
        check_vma=False,
    )
```

profile of v0, /device:TPU:1, one launch (start us, length us, event | category | flops | bytes accessed | tf_op | source)
XLA Modules:
  0.0 232.1 jit_solution(16710406030349881398)
XLA Ops:
  7.2 0.0 all-gather.2.cloned.1.call-start
  7.2 0.3 multiply_select_fusion.1
  7.6 0.1 broadcast_multiply_fusion
  7.7 0.1 mul.273
  7.8 4.2 %fusion.4 = f32[64,8192]{1,0:T(8,128)S(1)} fusion(f32[1,1,64,8192]{3,2,1,0:T(8,128)} %param.8, f32[1,1,64,8192]{3,2,1,0:T(8,128)} %param.7, f32[64]{0:T(128)S(1)} %add_multiply_fusion, pred[64]{0:T(512)(128)(4,1)S(1)} %iota_compare_fusion.9), kind=kOutput, calls=%fused_computation.6 | convolution fusion | flops 403722240 | bytes 6291776 | tf_op jit(solution)/shard_map/dot_general | solution.py:41
  12.0 1.5 reshape.192
  13.5 3.4 %fusion.38 = f32[4096,128]{1,0:T(8,128)S(1)} fusion(f32[4096,128]{1,0:T(8,128)} %reshape.192, f32[128,128]{1,0:T(8,128)S(1)} %mul.273), kind=kOutput, calls=%fused_computation.51 | convolution fusion | flops 805306368 | bytes 4259840 | tf_op jit(solution)/shard_map/dot_general | solution.py:43
  16.9 0.0 copy-start.1
  16.9 0.0 copy-start.2
  16.9 0.0 copy-start
  16.9 2.3 reshape_reshape.3
  19.2 0.0 copy-done.1
  19.2 0.1 copy.18
  19.4 0.0 copy-done.2
  19.4 0.1 fusion.22
  19.4 0.0 copy-done
  19.5 0.1 copy.17
  19.6 8.0 %fusion.2 = f32[128,4,64]{2,1,0:T(4,128)S(1)} fusion(f32[64,128,64]{2,1,0:T(8,128)} %reshape_reshape.3, f32[128,4]{1,0:T(8,128)S(1)} %fusion.22, s32[128,4]{1,0:T(8,128)S(1)} %copy.18), kind=kOutput, calls=%fused_computation.4 | convolution fusion | flops 25231360 | bytes 2232320 | tf_op jit(solution)/shard_map/ksf,fkg->ksg/dot_general | solution.py:75
  27.6 1.1 fusion.7
  28.7 1.2 fusion.39
  29.9 0.2 copy.20
  30.1 0.3 broadcast_in_dim.53
  30.4 31.9 %all_to_all.5 = f32[8,128,8,64]{1,3,2,0:T(8,128)S(1)} all-to-all(f32[8,128,8,64]{1,3,2,0:T(8,128)S(1)} %broadcast_in_dim.53), channel_id=1, replica_groups=mesh['row'=8,'col'=32] {'row'}, dimensions={0} | all-to-all | bytes 4194304 | tf_op jit(solution)/shard_map/all_to_all | solution.py:18
  62.3 0.1 reduce_sum.9
  62.4 0.8 copy.21
  63.3 0.0 all-gather.2.cloned.1.call-update
  63.3 39.0 %all_gather.7 = s32[32,128,8]{1,2,0:T(8,128)S(1)} all-gather(s32[1,128,8]{1,2,0:T(8,128)S(1)} %copy-done), channel_id=1, replica_groups=mesh['row'=8,'col'=32] {'col'}, dimensions={0}, use_global_device_ids=true | all-gather | bytes 135168 | tf_op jit(solution)/shard_map/all_gather | solution.py:84
  102.3 0.2 copy.23
  102.5 0.1 mul.276
  102.7 7.0 %fusion.8 = f32[128,64,64]{2,1,0:T(8,128)S(1)} fusion(f32[128,4,64]{2,1,0:T(4,128)S(1)} %fusion.2, f32[128,4]{1,0:T(8,128)S(1)} %fusion.22, s32[128,4]{1,0:T(8,128)S(1)} %copy.18), kind=kOutput, calls=%fused_computation.12 | convolution fusion | flops 25231360 | bytes 2232320 | tf_op jit(solution)/shard_map/ksf,ksg->fkg/dot_general | solution.py:76
  109.7 4.8 %fusion.23 = f32[64,8192]{1,0:T(8,128)S(1)} fusion(f32[64,8192]{0,1:T(8,128)S(1)} %bitcast.31, f32[64]{0:T(128)S(1)} %add_multiply_fusion, pred[64]{0:T(512)(128)(4,1)S(1)} %iota_compare_fusion.9), kind=kOutput, calls=%fused_computation.33 | convolution fusion | flops 402673664 | bytes 4194624 | tf_op jit(solution)/shard_map/dot_general | solution.py:51
  114.4 1.7 reshape.198
  116.2 3.4 %fusion.40 = f32[4096,128]{1,0:T(8,128)S(1)} fusion(f32[4096,128]{1,0:T(8,128)} %reshape.198, f32[128,128]{1,0:T(8,128)S(1)} %mul.276), kind=kOutput, calls=%fused_computation.53 | convolution fusion | flops 805306368 | bytes 4259840 | tf_op jit(solution)/shard_map/dot_general | solution.py:53
  119.6 1.5 reshape.199
  121.1 4.6 %fusion.6 = f32[1,1,64,8192]{3,2,1,0:T(8,128)} fusion(f32[1,1,64,8192]{3,2,1,0:T(8,128)} %reshape.199, f32[1,1,64,8192]{3,2,1,0:T(8,128)} %param.8, f32[1,1,64,8192]{3,2,1,0:T(8,128)} %param.7), kind=kLoop, calls=%fused_computation.9 | loop fusion | flops 1572864 | bytes 8388608 | tf_op jit(solution)/shard_map/sub | solution.py:77
  125.7 36.3 %all-gather.2.cloned.1.call-done = f32[32,128,512]{2,1,0:T(8,128)} async-done(((f32[1,128,512]{2,1,0:T(8,128)}), f32[32,128,512]{2,1,0:T(8,128)}) %all-gather.2.cloned.1.call-update) | async-done | bytes 8388624 | tf_op jit(solution)/shard_map/all_gather | solution.py:83
  162.0 8.9 %copy.22 = f32[32,128,512]{1,2,0:T(8,128)} copy(f32[32,128,512]{2,1,0:T(8,128)} %all-gather.2.cloned.1.call-done) | data formatting | bytes 16777216 | tf_op jit(solution)/shard_map/all_gather | solution.py:83
  171.0 16.2 %copy.24 = f32[32,128,8,64]{3,0,2,1:T(8,128)} copy(f32[32,128,8,64]{1,3,2,0:T(8,128)} %bitcast.29) | data formatting | bytes 16777216 | tf_op jit(solution)/shard_map/reshape | solution.py:86
  187.2 22.3 %fusion = f32[128,64,64,1]{2,1,3,0:T(8,128)S(1)} fusion(f32[32,128,8,64]{3,0,2,1:T(8,128)} %copy.24, s32[32,128,8]{0,2,1:T(8,128)S(1)} %copy.23), kind=kOutput, calls=%fused_computation.1 | convolution fusion | flops 1612709888 | bytes 10616832 | tf_op jit(solution)/shard_map/nkqf,nkqg->fkg/dot_general | solution.py:87
  209.5 4.7 %fusion.24 = f32[64,8192]{1,0:T(8,128)S(1)} fusion(f32[64,8192]{0,1:T(8,128)S(1)} %bitcast.30, f32[64]{0:T(128)S(1)} %add_multiply_fusion, pred[64]{0:T(512)(128)(4,1)S(1)} %iota_compare_fusion.9), kind=kOutput, calls=%fused_computation.34 | convolution fusion | flops 402673664 | bytes 4194624 | tf_op jit(solution)/shard_map/dot_general | solution.py:51
  214.2 1.5 reshape.196
  215.7 4.7 %convolution_multiply_fusion = f32[4096,128]{1,0:T(8,128)} fusion(f32[4096,128]{1,0:T(8,128)} %reshape.196, f32[128,128]{1,0:T(8,128)S(1)} %mul.276), kind=kOutput, calls=%fused_computation.3 | convolution fusion | flops 805830656 | bytes 4259840 | tf_op jit(solution)/shard_map/dot_general | solution.py:53
  220.4 1.7 mul.279
  222.2 3.1 %sub.7 = f32[64,8192]{1,0:T(8,128)} subtract(f32[64,8192]{1,0:T(8,128)} %param.6, f32[64,8192]{1,0:T(8,128)S(1)} %mul.279) | non-fusion elementwise | flops 524288 | bytes 6291456 | tf_op jit(solution)/shard_map/sub | solution.py:89
  (3 shorter events, 0.0 us)
Async XLA Ops:
  7.2 154.9 %all-gather.2.cloned.1.call-start = ((), (), s32[]{:S(2)}) async-start(), calls=%async_computation.1 | async-start | bytes 8650752 | tf_op jit(solution)/shard_map/all_gather | solution.py:83
  16.9 2.3 %copy-start.1 = (s32[1,1,128,4]{2,3,1,0:T(4,128)S(1)}, s32[1,1,128,4]{2,3,1,0:T(4,128)}, u32[]{:S(2)}) copy-start(s32[1,1,128,4]{2,3,1,0:T(4,128)} %param.9) | copy-start | bytes 6148
  16.9 2.4 %copy-start.2 = (s32[1,1,128]{2,1,0:T(1,128)S(1)}, s32[1,1,128]{2,1,0:T(1,128)}, u32[]{:S(2)}) copy-start(s32[1,1,128]{2,1,0:T(1,128)} %param.10) | copy-start | bytes 1540
  16.9 2.5 %copy-start = (s32[1,128,8]{1,2,0:T(8,128)S(1)}, s32[1,128,8]{1,2,0:T(8,128)}, u32[]{:S(2)}) copy-start(s32[1,128,8]{1,2,0:T(8,128)} %param.11) | copy-start | bytes 12292
Sparse Core Ops, SparseCore 0:
  63.4 98.5 all-gather.1
where the time goes:
time: 233 us; the launch traced here: 232 us
  blocking collectives  70.9 us (30%)
  matrix products  64.8 us (28%)
  local copies, waits for them, and re-layouts  37.5 us (16%)
  waiting for transfers between devices  36.3 us (16%)
  between operations  14.2 us (6%)
  other arithmetic  8.45 us (4%)
    all_gather x1, blocking collectives, body(): lists = lax.all_gather(common_rows, 'col', axis=0, tiled=True)  39 us
    all_gather x1, waiting for transfers between devices, body(): lax.all_gather(kept.reshape(1, blocks, -1), 'col', axis=0, tiled=True)  36.3 us
    all_to_all x1, blocking collectives, from_everyone(): lax.all_to_all(jnp.broadcast_to(array[None], (devices, *array.shape)), ax...  31.9 us
    dot_general x1, matrix products, body(): total = jnp.einsum('nkqf,nkqg->fkg', table, shaped, precision=highest)  22.3 us
    reshape x1, local copies, waits for them, and re-layouts, body(): shaped = vals.reshape(vals.shape[0], blocks, -1, CH)  16.2 us
    dot_general x2, matrix products, inverse(): jnp.dot(matrix.T, field, precision=highest, preferred_element_type=jnp.fl...  9.5 us
    all_gather x1, local copies, waits for them, and re-layouts, body(): lax.all_gather(kept.reshape(1, blocks, -1), 'col', axis=0, tiled=True)  8.95 us
    dot_general x2, matrix products, inverse(): jnp.dot(shaped, block_pair(matrix), precision=highest, preferred_element_...  8.11 us
  transfers between devices with their start and end apart: 1, of which 1 were waited for; matrix products, arithmetic and copies ran while one was open for 10% of the time, Pallas kernels for 0%

commit v1 on v0

v1 whole, which is shorter than its diff:
```python
import math

import jax
import jax.numpy as jnp
import numpy as np
from jax import lax
from jax.experimental import pallas as pl
from jax.experimental.pallas import tpu as pltpu
from jax.sharding import PartitionSpec as P

CH = 64
W = 8192
SPANS = 128
NY, NCORE, NZ, NX = 4, 2, 8, 4
PLANE = NY * NCORE * NX
OWN = W // PLANE
TILE = 1024
SUB = 256

decay_rate = 0.9
step_size = 0.1
MESH = pl.DeviceIdType.MESH
f32 = jnp.float32
bf16 = jnp.bfloat16


def dct_table(order):
    freq = np.arange(order)[:, None]
    place = np.arange(order)[None, :]
    matrix = math.sqrt(2.0 / order) * np.cos(math.pi * (2.0 * place + 1.0) * freq / (2.0 * order))
    return np.where(freq == 0, matrix * math.sqrt(0.5), matrix).astype(np.float32)


def table_parts():
    back = dct_table(CH).T
    high = back.astype(bf16)
    return high, (back - high.astype(np.float32)).astype(bf16)


def two_parts(value):
    high = value.astype(bf16)
    return high, (value - high.astype(f32)).astype(bf16)


def local_kernel(gather_ref, wanted_ref, chosen_ref, moment_ref, grad_ref, residual_ref, own_ref):
    freq = lax.broadcasted_iota(jnp.int32, (CH, 128), 0)
    hot = jnp.concatenate(
        [jnp.where(wanted_ref[0] == freq, 1.0, 0.0), jnp.where(chosen_ref[0] == freq, 1.0, 0.0)], axis=1
    ).astype(bf16)
    columns = jnp.dot(gather_ref[...], hot, preferred_element_type=f32)
    rows = columns.T.astype(bf16)
    back = columns[:, 128:].astype(bf16)
    back = jnp.concatenate([back[:64], back[:64], back[64:128]], axis=1)
    lane = lax.broadcasted_iota(jnp.int32, (8, 128), 1) < 64
    block_of_lane = lax.broadcasted_iota(jnp.int32, (32, SUB), 1) // 64
    block_of_row = lax.broadcasted_iota(jnp.int32, (32, SUB), 0) // 8
    same = block_of_lane == block_of_row
    for i in range(TILE // SUB):
        at = pl.ds(i * SUB, SUB)
        x = decay_rate * moment_ref[:, at] + grad_ref[:, at]
        xh, xl = two_parts(x)
        left = jnp.concatenate([rows[32 * i : 32 * i + 32], rows[128 + 32 * i : 160 + 32 * i]], axis=0)
        picked = jnp.dot(left, jnp.concatenate([xh, xh, xl], axis=0), preferred_element_type=f32)
        for h in range(2):
            part = picked[16 * h : 16 * h + 16, 128 * h : 128 * h + 128]
            own_ref[:, pl.ds(i * SUB + 128 * h, 128)] = jnp.where(lane, part[:8], part[8:])
        values = jnp.where(same, picked[32:], 0.0)
        vh, vl = two_parts(values)
        above = [jnp.zeros((32 * i, SUB), bf16)] if i else []
        below = [jnp.zeros((96 - 32 * i, SUB), bf16)] if i < 3 else []
        stack = jnp.concatenate(
            above + [vh] + below + above + [vl] + below + above + [vh] + below, axis=0
        )
        residual_ref[:, at] = x - jnp.dot(back, stack, preferred_element_type=f32)


def local_part(gather, wanted, chosen, moment, grads):
    tiles = W // TILE
    small = pl.BlockSpec((1, 1, 128), lambda t: (t, 0, 0))
    wide = pl.BlockSpec((CH, TILE), lambda t: (0, t))
    return pl.pallas_call(
        local_kernel,
        grid=(tiles,),
        in_specs=[pl.BlockSpec((192, CH), lambda t: (0, 0)), small, small, wide, wide],
        out_specs=[wide, pl.BlockSpec((8, TILE), lambda t: (0, t))],
        out_shape=[jax.ShapeDtypeStruct((CH, W), f32), jax.ShapeDtypeStruct((8, W), f32)],
        name="local_part",
    )(gather, wanted, chosen, moment, grads)


def exchange_kernel(
    own_ref, names_ref, inverse_ref, params_ref, out_ref,
    parts, values, names, mine,
    param_sem, name_send, name_recv, row_send, row_recv, deep_send, deep_recv,
    first_send, first_recv, second_send, second_recv, pair_send, pair_recv,
):
    r = lax.axis_index("row")
    c = lax.axis_index("col")
    z, x = c // NX, lax.rem(c, NX)
    y, core = r // NCORE, lax.rem(r, NCORE)
    m = r * NX + x

    def in_plane(index):
        return (index // NX, z * NX + lax.rem(index, NX))

    def along_x(d):
        return (r, z * NX + lax.rem(x + d, NX))

    def along_y(d):
        return (lax.rem(y + d, NY) * NCORE + core, c)

    def along_z(d):
        return (r, lax.rem(z + d, NZ) * NX + x)

    def lanes(index, size):
        return pl.ds(pl.multiple_of(index * size, size), size)

    def remote(src, dst, send, recv, device):
        return pltpu.make_async_remote_copy(
            src_ref=src, dst_ref=dst, send_sem=send, recv_sem=recv, device_id=device, device_id_type=MESH
        )

    params_in = pltpu.make_async_copy(params_ref.at[:, lanes(m, OWN)], mine, param_sem)
    params_in.start()
    barrier = pltpu.get_barrier_semaphore()

    def greet_plane(d, carry):
        pl.semaphore_signal(barrier, inc=1, device_id=in_plane(lax.rem(m + d, PLANE)), device_id_type=MESH)
        return carry

    def greet_deep(d, carry):
        pl.semaphore_signal(barrier, inc=1, device_id=along_z(d), device_id_type=MESH)
        return carry

    lax.fori_loop(1, PLANE, greet_plane, 0)
    lax.fori_loop(1, NZ, greet_deep, 0)
    names[z, x] = names_ref[:, lanes(m, 128)]
    parts[m] = own_ref[:, lanes(m, OWN)]
    pl.semaphore_wait(barrier, PLANE - 1 + NZ - 1)

    for d in range(1, NX):
        there = r * NX + lax.rem(x + d, NX)
        remote(names_ref.at[:, lanes(there, 128)], names.at[z, x], name_send.at[0], name_recv.at[0], along_x(d)).start()

    def send_part(d, carry):
        there = lax.rem(m + d, PLANE)
        remote(own_ref.at[:, lanes(there, OWN)], parts.at[m], row_send, row_recv, in_plane(there)).start()
        return carry

    lax.fori_loop(1, PLANE, send_part, 0)
    some = names.at[0, pl.ds(0, NX - 1)]
    arrived = remote(some, some, name_send.at[0], name_recv.at[0], along_x(1))
    arrived.wait_recv()

    def send_names(d, carry):
        remote(names.at[z], names.at[z], name_send.at[1], name_recv.at[1], along_z(d)).start()
        return carry

    lax.fori_loop(1, NZ, send_names, 0)
    some = parts.at[pl.ds(0, PLANE - 1)]
    rows_moved = remote(some, some, row_send, row_recv, along_x(1))
    rows_moved.wait_recv()
    for group in range(NX):
        total = parts[group]
        for other in range(1, NY * NCORE):
            total = total + parts[other * NX + group]
        values[z, group] = total

    def send_values(d, carry):
        remote(values.at[z], values.at[z], deep_send, deep_recv, along_z(d)).start()
        return carry

    lax.fori_loop(1, NZ, send_values, 0)
    some = names.at[pl.ds(0, NZ - 1)]
    names_moved = remote(some, some, name_send.at[1], name_recv.at[1], along_z(1))
    names_moved.wait_recv()
    listed = names[...].reshape(NZ * NX * 8, 128)
    lane = lax.broadcasted_iota(jnp.int32, (NZ * NX * 8, 128), 1)
    freq = lax.rem(lane, CH)
    spreads = []
    for h in range(2):
        first = jnp.broadcast_to(listed[:, 64 * h : 64 * h + 1], lane.shape)
        second = jnp.broadcast_to(listed[:, 64 * h + 32 : 64 * h + 33], lane.shape)
        hot = jnp.where(jnp.where(lane < CH, first, second) == freq, 1.0, 0.0)
        spreads.append(hot.T.astype(bf16))
    some = values.at[pl.ds(0, NZ - 1)]
    deep_moved = remote(some, some, deep_send, deep_recv, along_z(1))
    deep_moved.wait_recv()
    gathered = values[...].reshape(NZ * NX * 8, OWN)
    left = lax.broadcasted_iota(jnp.int32, (CH, 128), 1) < CH
    totals = []
    for h in range(2):
        high, low = two_parts(gathered[:, 128 * h : 128 * h + 128])
        both = jnp.dot(spreads[h], high, preferred_element_type=f32)
        both = both + jnp.dot(spreads[h], low, preferred_element_type=f32)
        totals.append(jnp.where(left, both[:CH], both[CH:]))
    high, low = two_parts(jnp.concatenate(totals, axis=1))
    update = jnp.dot(inverse_ref[...], jnp.concatenate([high, high, low], axis=0), preferred_element_type=f32)
    params_in.wait()
    out_ref[:, lanes(m, OWN)] = mine[...] - step_size * update

    started = []

    def go(copy):
        copy.start()
        started.append(copy)
        return copy

    def place(half, index):
        return out_ref.at[pl.ds(32 * half, 32), lanes(index, OWN)]

    def send(half, index, sems, slot, device):
        at = place(half, index)
        return go(remote(at, at, sems[0].at[slot], sems[1].at[slot], device))

    first = (first_send, first_recv)
    second = (second_send, second_recv)
    partner = (y * NCORE + (1 - core), c)

    def to_partner(half, index):
        at = place(half, index)
        go(remote(at, at, pair_send, pair_recv, partner))

    def at_x(d):
        return r * NX + lax.rem(x + NX - d, NX)

    def at_y(d):
        return (lax.rem(y + NY - d, NY) * NCORE + core) * NX + x

    def at_both(dy, dx):
        return (lax.rem(y + NY - dy, NY) * NCORE + core) * NX + lax.rem(x + NX - dx, NX)

    one = [send(0, m, first, d - 1, along_x(d)) for d in range(1, NX)]
    two = [send(1, m, first, 2 + d, along_y(d)) for d in range(1, NY)]
    over_y = [[None] * NX for _ in range(NY)]
    over_x = [[None] * NY for _ in range(NX)]
    for d in range(1, NY):
        over_y[d][0] = send(0, m, second, (d - 1) * NX, along_y(d))
    for d in range(1, NX):
        over_x[d][0] = send(1, m, second, 12 + (d - 1) * NY, along_x(d))
    to_partner(0, m)
    to_partner(1, m)
    for j in range(1, 4):
        one[j - 1].wait_recv()
        for d in range(1, NY):
            over_y[d][j] = send(0, at_x(j), second, (d - 1) * NX + j, along_y(d))
        to_partner(0, at_x(j))
        two[j - 1].wait_recv()
        for d in range(1, NX):
            over_x[d][j] = send(1, at_y(j), second, 12 + (d - 1) * NY + j, along_x(d))
        to_partner(1, at_y(j))
    for j in range(4):
        for d in range(1, 4):
            over_y[d][j].wait_recv()
            to_partner(0, at_both(d, j))
            over_x[d][j].wait_recv()
            to_partner(1, at_both(j, d))
    some = out_ref.at[:, pl.ds(0, W // 2)]
    remote(some, some, pair_send, pair_recv, partner).wait_recv()
    for copy in started:
        copy.wait_send()
    arrived.wait_send()
    rows_moved.wait_send()
    names_moved.wait_send()
    deep_moved.wait_send()


def exchange(own, names, inverse, params):
    vmem = pl.BlockSpec(memory_space=pltpu.VMEM)
    dma = pltpu.SemaphoreType.DMA
    return pl.pallas_call(
        exchange_kernel,
        out_shape=jax.ShapeDtypeStruct((CH, W), f32),
        in_specs=[vmem, vmem, vmem, pl.BlockSpec(memory_space=pl.ANY)],
        out_specs=vmem,
        scratch_shapes=[
            pltpu.VMEM((PLANE, 8, OWN), f32),
            pltpu.VMEM((NZ, NX, 8, OWN), f32),
            pltpu.VMEM((NZ, NX, 8, 128), jnp.int32),
            pltpu.VMEM((CH, OWN), f32),
            dma, dma((2,)), dma((2,)), dma, dma, dma, dma,
            dma((6,)), dma((6,)), dma((24,)), dma((24,)), dma, dma,
        ],
        compiler_params=pltpu.CompilerParams(collective_id=0, has_side_effects=True),
        name="exchange",
    )(own, names, inverse, params)


def body(params, momentum, gradient, chosen_rows, live_counts, common_rows):
    chosen, counts, common = chosen_rows[0, 0], live_counts[0, 0], common_rows[0]
    live = jnp.arange(chosen.shape[1], dtype=jnp.int32) < counts[:, None]
    chosen = jnp.where(live, chosen, -1)
    found = jnp.any(common[:, :, None] == chosen[:, None, :], axis=-1)
    wanted = jnp.where(found, common, -1)
    chosen = jnp.concatenate([chosen, jnp.full_like(chosen, -1)], axis=1)
    names = jnp.repeat(common.T, 32, axis=1)
    high, low = table_parts()
    gather = jnp.asarray(np.concatenate([high, low, high], axis=0))
    inverse = jnp.asarray(np.concatenate([high, low, high], axis=1))
    residual, own = local_part(
        gather, wanted.reshape(8, 1, 128), chosen.reshape(8, 1, 128), momentum[0, 0], gradient[0, 0]
    )
    new_params = exchange(own, names, inverse, params)
    return (new_params, residual[None, None])


def solution(mesh):
    placed = (
        P(),
        P("row", "col", None, None),
        P("row", "col", None, None),
        P("row", "col", None, None),
        P("row", "col", None),
        P("col", None, None),
    )
    return jax.shard_map(
        body,
        mesh=mesh,
        in_specs=placed,
        out_specs=(P(), P("row", "col", None, None)),
        check_vma=False,
    )
```

time: 233 us -> 59.7 us (0.26)
  blocking collectives: 70.9 us -> 0 us
  matrix products: 64.8 us -> 0 us
  Pallas kernels: 0 us -> 49.9 us
  waiting for transfers between devices: 36.3 us -> 0 us
  local copies, waits for them, and re-layouts: 37.5 us -> 6.74 us
  between operations: 14.2 us -> 0.65 us
  other arithmetic: 8.45 us -> 1.99 us
    dot_general x11 -> x0, matrix products: 64.8 us -> none  [the longest x1 22.3 us: body(): total = jnp.einsum('nkqf,nkqg->fkg', table, shaped, precision=highest)]
    pallas_call x0 -> x2, Pallas kernels: none -> 49.9 us  [the longest x1 40.8 us: exchange(): pl.pallas_call(exchange_kernel, out_shape=jax.ShapeDtypeStruct((CH, W), f...]
    all_gather x1 -> x0, blocking collectives: 39 us -> none  [body(): lists = lax.all_gather(common_rows, 'col', axis=0, tiled=True)]
    all_gather x1 -> x0, waiting for transfers between devices: 36.3 us -> none  [body(): lax.all_gather(kept.reshape(1, blocks, -1), 'col', axis=0, tiled=True)]
    all_to_all x1 -> x0, blocking collectives: 31.9 us -> none  [from_everyone(): lax.all_to_all(jnp.broadcast_to(array[None], (devices, *array.shape)), ax...]
    reshape x6 -> x2, local copies, waits for them, and re-layouts: 23.3 us -> 1.57 us  [the longest x1 0.89 us: body(): names = jnp.repeat(common.T, 32, axis=1)]
    all_gather x2 -> x0, local copies, waits for them, and re-layouts: 9.2 us -> none  [the longest x1 8.95 us: body(): lax.all_gather(kept.reshape(1, blocks, -1), 'col', axis=0, tiled=True)]
    sub x2 -> x0, other arithmetic: 7.76 us -> none  [the longest x1 4.64 us: body(): residual = decayed - inverse(sent.reshape(CH, -1))]
  transfers between devices with their start and end apart: 1 -> 0, of which waited for: 1 -> 0; matrix products, arithmetic and copies ran while one was open for 10% -> 0% of each run, Pallas kernels for 0% -> 0%
where the time goes in v1:
time: 59.7 us; the launch traced here: 59.3 us
  Pallas kernels  49.9 us (84%)
  local copies, waits for them, and re-layouts  6.74 us (11%)
  other arithmetic  1.99 us (3%)
  between operations  0.65 us (1%)
    pallas_call x1, Pallas kernels, exchange(): pl.pallas_call(exchange_kernel, out_shape=jax.ShapeDtypeStruct((CH, W), f...  40.8 us
    pallas_call x1, Pallas kernels, local_part(): pl.pallas_call(local_kernel, grid=(tiles,), in_specs=[pl.BlockSpec((192,...  9.08 us
    unnamed x3, local copies, waits for them, and re-layouts  3.96 us

profile of v1, /device:TPU:1, one launch (start us, length us, event | category | flops | bytes accessed | tf_op | source)
XLA Modules:
  0.0 59.3 jit_solution(18319541922051781647)
XLA Ops:
  0.6 0.7 %bitcast_select_fusion = s32[128,4]{0,1:T(4,128)S(1)} fusion(s32[1,1,128,4]{2,3,1,0:T(4,128)} %param.11, s32[128]{0:T(128)} %bitcast.17), kind=kLoop, calls=%fused_computation.1 | loop fusion | flops 1024 | bytes 4608 | tf_op jit(solution)/shard_map/jit(_where)/select_n | solution.py:292
  1.3 0.7 %compare_reduce_fusion = pred[128,8]{0,1:T(8,128)(4,1)S(1)} fusion(s32[128,4]{0,1:T(4,128)S(1)} %bitcast_select_fusion, s32[128,8]{0,1:T(8,128)} %bitcast.13), kind=kLoop, calls=%fused_computation | loop fusion | flops 7168 | bytes 7168 | tf_op jit(solution)/shard_map/reduce_or | solution.py:293
  2.0 0.1 copy.21
  2.1 0.1 reduce_or.13
  2.2 0.1 copy.27
  2.4 0.7 %reshape.54 = s32[8,1,128]{2,0,1:T(8,128)} reshape(s32[128,8]{1,0:T(8,128)S(1)} %concatenate.3.clone) | data formatting | bytes 8192 | tf_op jit(solution)/shard_map/reshape | solution.py:301
  3.0 0.8 %copy.22 = s32[1,128,8]{2,1,0:T(8,128)S(1)} copy(s32[1,128,8]{1,2,0:T(8,128)} %param.13) | data formatting | bytes 8192 | tf_op args[5]
  3.8 0.1 squeeze.13
  3.9 0.6 %broadcast_select_fusion.wanted_ref = s32[8,1,128]{2,1,0:T(1,128)} fusion(pred[8,1,128]{2,1,0:T(4,128)(4,1)S(1)} %reduce_or.13, s32[8,1,128]{2,1,0:T(1,128)S(1)} %bitcast.15), kind=kLoop, calls=%fused_computation.2 | loop fusion | flops 1024 | bytes 9216 | tf_op jit(solution)/shard_map/jit(_where)/select_n | solution.py:294
  4.5 0.9 %broadcast_in_dim.19 = s32[8,128,32]{2,1,0:T(8,128)S(1)} broadcast(s32[8,128]{1,0:T(8,128)} %bitcast.14), dimensions={0,1} | broadcast | bytes 135168 | tf_op jit(solution)/shard_map/broadcast_in_dim | solution.py:296
  5.4 0.9 %reshape.55.names_ref = s32[8,4096]{1,0:T(8,128)} reshape(s32[8,128,32]{2,1,0:T(8,128)S(1)} %broadcast_in_dim.19) | data formatting | bytes 262144 | tf_op jit(solution)/shard_map/reshape | solution.py:296
  6.3 9.1 %local_part.1 = (f32[64,8192]{1,0:T(8,128)}, f32[8,8192]{1,0:T(8,128)}) custom-call(bf16[192,64]{1,0:T(8,128)(2,1)} %constant.3.clone.gather_ref, s32[8,1,128]{2,1,0:T(1,128)} %broadcast_select_fusion.wanted_ref, s32[8,1,128]{2,1,0:T(1,128)} %bitcast.16, f32[64,8192]{1,0:T(8,128)} %bitcast.11, f32[64,8192]{1,0:T(8,128)} %bitcast.12), custom_call_target="tpu_custom_call" | custom-call | tf_op jit(solution)/shard_map/local_part/pallas_call | solution.py:81
  15.4 40.8 %exchange.1 = f32[64,8192]{1,0:T(8,128)} custom-call(f32[8,8192]{1,0:T(8,128)} %get-tuple-element.4.own_ref, s32[8,4096]{1,0:T(8,128)} %reshape.55.names_ref, bf16[64,192]{1,0:T(8,128)(2,1)} %constant.10.clone.inverse_ref, f32[64,8192]{1,0:T(8,128)} %params_ref.1), custom_call_target="tpu_custom_call" | custom-call | tf_op jit(solution)/shard_map/exchange/pallas_call | solution.py:271
  56.2 3.1 %copy.29 = f32[64,8192]{1,0:T(8,128)} copy(f32[64,8192]{1,0:T(8,128)} %exchange.1) | data formatting | bytes 4194304
  (1 shorter events, 0.0 us)

commit v2 on v1

v2 whole, which is shorter than its diff:
```python
import math

import jax
import jax.numpy as jnp
import numpy as np
from jax import lax
from jax.experimental import pallas as pl
from jax.experimental.pallas import tpu as pltpu
from jax.sharding import PartitionSpec as P

CH = 64
W = 8192
SPANS = 128
S = 4
Q = 8
NY, NCORE, NZ, NX = 4, 2, 8, 4
PLANE = NY * NCORE * NX
OWN = W // PLANE
TILE = 1024
TILES = W // TILE
SUB = 256
VMEM_GRANT = 67043328 - 2 * 4 * CH * W - 4096

decay_rate = 0.9
step_size = 0.1
MESH = pl.DeviceIdType.MESH
f32 = jnp.float32
bf16 = jnp.bfloat16


def dct_table(order):
    freq = np.arange(order)[:, None]
    place = np.arange(order)[None, :]
    matrix = math.sqrt(2.0 / order) * np.cos(math.pi * (2.0 * place + 1.0) * freq / (2.0 * order))
    return np.where(freq == 0, matrix * math.sqrt(0.5), matrix).astype(np.float32)


def table_parts():
    back = dct_table(CH).T
    high = back.astype(bf16)
    return high, (back - high.astype(np.float32)).astype(bf16)


def two_parts(value):
    high = value.astype(bf16)
    return high, (value - high.astype(f32)).astype(bf16)


def step_kernel(
    gather_hbm, inverse_hbm, common_hbm, chosen_hbm, counts_hbm, moment_ref, grad_ref, params_ref,
    out_ref, residual_ref,
    gather_ref, inverse_ref, common_ref, chosen_ref, counts_ref, small_sem,
    decayed, grads, hot_wanted, hot_chosen, wanted_rows, chosen_rows, chosen_values, own, parts, values, names, mine,
    moment_sem, grad_sem, param_sem, name_send, name_recv, row_send, row_recv, deep_send, deep_recv,
    first_send, first_recv, second_send, second_recv, pair_send, pair_recv,
):
    r = lax.axis_index("row")
    c = lax.axis_index("col")
    z, x = c // NX, lax.rem(c, NX)
    y, core = r // NCORE, lax.rem(r, NCORE)
    m = r * NX + x

    def in_plane(index):
        return (index // NX, z * NX + lax.rem(index, NX))

    def along_x(d):
        return (r, z * NX + lax.rem(x + d, NX))

    def along_y(d):
        return (lax.rem(y + d, NY) * NCORE + core, c)

    def along_z(d):
        return (r, lax.rem(z + d, NZ) * NX + x)

    def lanes(index, size):
        return pl.ds(pl.multiple_of(index * size, size), size)

    def half_lanes(index, h):
        return pl.ds(pl.multiple_of(index * OWN + 128 * h, 128), 128)

    def remote(src, dst, send, recv, device):
        return pltpu.make_async_remote_copy(
            src_ref=src, dst_ref=dst, send_sem=send, recv_sem=recv, device_id=device, device_id_type=MESH
        )

    def moment_in(t):
        return pltpu.make_async_copy(moment_ref.at[:, lanes(t, TILE)], decayed.at[:, lanes(t, TILE)], moment_sem.at[t])

    def grad_in(t):
        return pltpu.make_async_copy(grad_ref.at[:, lanes(t, TILE)], grads.at[:, lanes(t, TILE)], grad_sem.at[t])

    smalls = [
        pltpu.make_async_copy(src, dst, small_sem.at[i])
        for i, (src, dst) in enumerate(
            [
                (chosen_hbm, chosen_ref),
                (counts_hbm, counts_ref),
                (common_hbm, common_ref),
                (gather_hbm, gather_ref),
                (inverse_hbm, inverse_ref),
            ]
        )
    ]
    for copy in smalls:
        copy.start()
    for t in range(TILES):
        moment_in(t).start()
        grad_in(t).start()
    params_in = pltpu.make_async_copy(params_ref.at[:, lanes(m, OWN)], mine, param_sem)
    params_in.start()
    barrier = pltpu.get_barrier_semaphore()

    def greet_plane(d, carry):
        pl.semaphore_signal(barrier, inc=1, device_id=in_plane(lax.rem(m + d, PLANE)), device_id_type=MESH)
        return carry

    def greet_deep(d, carry):
        pl.semaphore_signal(barrier, inc=1, device_id=along_z(d), device_id_type=MESH)
        return carry

    lax.fori_loop(1, NZ, greet_deep, 0)
    lax.fori_loop(1, PLANE, greet_plane, 0)

    for copy in smalls:
        copy.wait()
    common = common_ref[...]
    place = lax.broadcasted_iota(jnp.int32, (S, SPANS), 0)
    chosen = jnp.where(place < counts_ref[...], chosen_ref[...], -1)
    found = common == chosen[0:1]
    for s in range(1, S):
        found = found | (common == chosen[s : s + 1])
    wanted = jnp.where(found, common, -1)
    freq = lax.broadcasted_iota(jnp.int32, (128, SPANS), 0)
    for q in range(Q):
        hot_wanted[pl.ds(q, SPANS, stride=Q), :] = jnp.where(wanted[q : q + 1] == freq, 1.0, 0.0).T
    for s in range(S):
        hot_chosen[pl.ds(s, SPANS, stride=S), :] = jnp.where(chosen[s : s + 1] == freq, 1.0, 0.0).T
    wanted_rows[...] = jnp.dot(
        hot_wanted[...].astype(bf16), gather_ref[...], preferred_element_type=f32
    ).astype(bf16)
    chosen_rows[...] = jnp.dot(hot_chosen[...].astype(bf16), gather_ref[...], preferred_element_type=f32)
    names[z, x] = common
    left_lane = lax.broadcasted_iota(jnp.int32, (8, 128), 1) < CH

    def local_sums(t, carry):
        moment_in(t).wait()
        grad_in(t).wait()
        for i in range(TILE // SUB):
            at = pl.ds(pl.multiple_of(t * TILE + i * SUB, SUB), SUB)
            field = decay_rate * decayed[:, at] + grads[:, at]
            decayed[:, at] = field
            high, low = two_parts(field)
            step = t * (TILE // SUB) + i
            left = jnp.concatenate(
                [
                    wanted_rows[pl.ds(pl.multiple_of(step * 4 * Q, 4 * Q), 4 * Q), :],
                    chosen_rows[pl.ds(pl.multiple_of(step * 4 * S, 4 * S), 4 * S), :].astype(bf16),
                ],
                axis=0,
            )
            picked = jnp.dot(left, jnp.concatenate([high, high, low], axis=0), preferred_element_type=f32)
            for h in range(2):
                part = picked[16 * h : 16 * h + 16, 128 * h : 128 * h + 128]
                own[:, pl.ds(pl.multiple_of(t * TILE + i * SUB + 128 * h, 128), 128)] = jnp.where(
                    left_lane, part[:8], part[8:]
                )
            chosen_values[:, at] = picked[4 * Q :]
        return carry

    lax.fori_loop(0, TILES, local_sums, 0)
    pl.semaphore_wait(barrier, PLANE - 1 + NZ - 1)

    for d in range(1, NX):
        remote(common_ref, names.at[z, x], name_send.at[0], name_recv.at[0], along_x(d)).start()
    for h in range(2):

        def send_part(d, carry):
            there = lax.rem(m + d, PLANE)
            remote(
                own.at[:, half_lanes(there, h)], parts.at[h, m], row_send.at[h], row_recv.at[h], in_plane(there)
            ).start()
            return carry

        lax.fori_loop(1, PLANE, send_part, 0)
        parts[h, m] = own[:, half_lanes(m, h)]
    some = names.at[0, pl.ds(0, NX - 1)]
    near_names = remote(some, some, name_send.at[0], name_recv.at[0], along_x(1))
    near_names.wait_recv()

    def send_names(d, carry):
        remote(names.at[z], names.at[z], name_send.at[1], name_recv.at[1], along_z(d)).start()
        return carry

    lax.fori_loop(1, NZ, send_names, 0)

    same = lax.broadcasted_iota(jnp.int32, (4 * S, SUB), 1) // CH == lax.broadcasted_iota(jnp.int32, (4 * S, SUB), 0) // S

    def residuals(t, carry):
        for i in range(TILE // SUB):
            at = pl.ds(pl.multiple_of(t * TILE + i * SUB, SUB), SUB)
            step = t * (TILE // SUB) + i
            rows = chosen_rows[pl.ds(pl.multiple_of(step * 4 * S, 4 * S), 4 * S), :]
            back = jnp.concatenate([rows[:, :CH], rows[:, :CH], rows[:, CH : 2 * CH]], axis=0).T.astype(bf16)
            high, low = two_parts(jnp.where(same, chosen_values[:, at], 0.0))
            sent = jnp.dot(back, jnp.concatenate([high, low, high], axis=0), preferred_element_type=f32)
            residual_ref[:, at] = decayed[:, at] - sent
        return carry

    lax.fori_loop(0, TILES, residuals, 0)

    rows_moved = []
    for h in range(2):
        some = parts.at[h, pl.ds(0, PLANE - 1)]
        moved = remote(some, some, row_send.at[h], row_recv.at[h], along_x(1))
        moved.wait_recv()
        rows_moved.append(moved)
        for group in range(NX):
            total = parts[h, group]
            for other in range(1, NY * NCORE):
                total = total + parts[h, other * NX + group]
            values[h, z, group] = total

        def send_values(d, carry):
            remote(values.at[h, z], values.at[h, z], deep_send.at[h], deep_recv.at[h], along_z(d)).start()
            return carry

        lax.fori_loop(1, NZ, send_values, 0)

    some = names.at[pl.ds(0, NZ - 1)]
    far_names = remote(some, some, name_send.at[1], name_recv.at[1], along_z(1))
    far_names.wait_recv()
    listed = names[...].reshape(NZ * NX * Q, SPANS).astype(f32).astype(bf16)
    lane = lax.broadcasted_iota(jnp.int32, (128, 128), 1)
    block = lax.broadcasted_iota(jnp.int32, (128, 128), 0)
    wide_lane = lax.broadcasted_iota(jnp.int32, (NZ * NX * Q, 128), 1)
    wide_freq = lax.rem(wide_lane, CH).astype(f32)
    spreads = []
    for h in range(2):
        pick = jnp.where(block == m * 4 + 2 * h + lane // CH, 1.0, 0.0).astype(bf16)
        spread_names = jnp.dot(listed, pick, preferred_element_type=f32)
        spreads.append(jnp.where(spread_names == wide_freq, 1.0, 0.0).T.astype(bf16))
    params_in.wait()
    left = lax.broadcasted_iota(jnp.int32, (CH, 128), 1) < CH

    started = []

    def go(copy):
        copy.start()
        started.append(copy)
        return copy

    def place_of(h, rows, index):
        return out_ref.at[pl.ds(32 * rows, 32), half_lanes(index, h)]

    def send(h, rows, index, sems, slot, device):
        at = place_of(h, rows, index)
        return go(remote(at, at, sems[0].at[h, slot], sems[1].at[h, slot], device))

    first = (first_send, first_recv)
    second = (second_send, second_recv)
    partner = (y * NCORE + (1 - core), c)

    def to_partner(h, rows, index):
        at = place_of(h, rows, index)
        go(remote(at, at, pair_send, pair_recv, partner))

    def at_x(d):
        return r * NX + lax.rem(x + NX - d, NX)

    def at_y(d):
        return (lax.rem(y + NY - d, NY) * NCORE + core) * NX + x

    def at_both(dy, dx):
        return (lax.rem(y + NY - dy, NY) * NCORE + core) * NX + lax.rem(x + NX - dx, NX)

    deep_moved = []
    over = []
    for h in range(2):
        some = values.at[h, pl.ds(0, NZ - 1)]
        moved = remote(some, some, deep_send.at[h], deep_recv.at[h], along_z(1))
        moved.wait_recv()
        deep_moved.append(moved)
        high, low = two_parts(values[h].reshape(NZ * NX * Q, 128))
        both = jnp.dot(spreads[h], high, preferred_element_type=f32)
        both = both + jnp.dot(spreads[h], low, preferred_element_type=f32)
        high, low = two_parts(jnp.where(left, both[:CH], both[CH:]))
        update = jnp.dot(inverse_ref[...], jnp.concatenate([high, high, low], axis=0), preferred_element_type=f32)
        out_ref[:, half_lanes(m, h)] = mine[:, 128 * h : 128 * h + 128] - step_size * update
        one = [send(h, 0, m, first, d - 1, along_x(d)) for d in range(1, NX)]
        two = [send(h, 1, m, first, 2 + d, along_y(d)) for d in range(1, NY)]
        over_y = [[None] * NX for _ in range(NY)]
        over_x = [[None] * NY for _ in range(NX)]
        for d in range(1, NY):
            over_y[d][0] = send(h, 0, m, second, (d - 1) * NX, along_y(d))
        for d in range(1, NX):
            over_x[d][0] = send(h, 1, m, second, 12 + (d - 1) * NY, along_x(d))
        to_partner(h, 0, m)
        to_partner(h, 1, m)
        over.append((one, two, over_y, over_x))
    for h in range(2):
        one, two, over_y, over_x = over[h]
        for j in range(1, 4):
            one[j - 1].wait_recv()
            for d in range(1, NY):
                over_y[d][j] = send(h, 0, at_x(j), second, (d - 1) * NX + j, along_y(d))
            to_partner(h, 0, at_x(j))
            two[j - 1].wait_recv()
            for d in range(1, NX):
                over_x[d][j] = send(h, 1, at_y(j), second, 12 + (d - 1) * NY + j, along_x(d))
            to_partner(h, 1, at_y(j))
    for h in range(2):
        one, two, over_y, over_x = over[h]
        for j in range(4):
            for d in range(1, 4):
                over_y[d][j].wait_recv()
                to_partner(h, 0, at_both(d, j))
                over_x[d][j].wait_recv()
                to_partner(h, 1, at_both(j, d))
    some = out_ref.at[:, pl.ds(0, W // 2)]
    remote(some, some, pair_send, pair_recv, partner).wait_recv()
    for copy in started + rows_moved + deep_moved + [near_names, far_names]:
        copy.wait_send()


def step(gather, inverse, common, chosen, counts, momentum, gradient, params):
    vmem = pl.BlockSpec(memory_space=pltpu.VMEM)
    outside = pl.BlockSpec(memory_space=pltpu.HBM)
    dma = pltpu.SemaphoreType.DMA
    return pl.pallas_call(
        step_kernel,
        out_shape=(pltpu.VMEM((CH, W), f32), pltpu.VMEM((CH, W), f32)),
        in_specs=[outside] * 8,
        out_specs=(vmem, vmem),
        scratch_shapes=[
            pltpu.VMEM((128, 3 * CH), bf16),
            pltpu.VMEM((CH, 3 * CH), bf16),
            pltpu.VMEM((Q, SPANS), jnp.int32),
            pltpu.VMEM((S, SPANS), jnp.int32),
            pltpu.VMEM((1, SPANS), jnp.int32),
            dma((5,)),
            pltpu.VMEM((CH, W), f32),
            pltpu.VMEM((CH, W), f32),
            pltpu.VMEM((SPANS * Q, 128), f32),
            pltpu.VMEM((SPANS * S, 128), f32),
            pltpu.VMEM((SPANS * Q, 3 * CH), bf16),
            pltpu.VMEM((SPANS * S, 3 * CH), f32),
            pltpu.VMEM((4 * S, W), f32),
            pltpu.VMEM((Q, W), f32),
            pltpu.VMEM((2, PLANE, Q, 128), f32),
            pltpu.VMEM((2, NZ, NX, Q, 128), f32),
            pltpu.VMEM((NZ, NX, Q, SPANS), jnp.int32),
            pltpu.VMEM((CH, OWN), f32),
            dma((TILES,)), dma((TILES,)), dma, dma((2,)), dma((2,)), dma((2,)), dma((2,)), dma((2,)), dma((2,)),
            dma((2, 6)), dma((2, 6)), dma((2, 24)), dma((2, 24)), dma, dma,
        ],
        compiler_params=pltpu.CompilerParams(collective_id=0, has_side_effects=True, vmem_limit_bytes=VMEM_GRANT),
        name="step",
    )(gather, inverse, common, chosen, counts, momentum, gradient, params)


def deliver_kernel(first_ref, second_ref, first_out, second_out, sems):
    copies = []
    for t in range(TILES):
        for i, (src, dst) in enumerate([(first_ref, first_out), (second_ref, second_out)]):
            at = pl.ds(t * TILE, TILE)
            copies.append(pltpu.make_async_copy(src.at[:, at], dst.at[:, at], sems.at[i, t]))
    for copy in copies:
        copy.start()
    for copy in copies:
        copy.wait()


def deliver(first, second):
    vmem = pl.BlockSpec(memory_space=pltpu.VMEM)
    outside = pl.BlockSpec(memory_space=pltpu.HBM)
    shape = jax.ShapeDtypeStruct((CH, W), f32)
    return pl.pallas_call(
        deliver_kernel,
        out_shape=(shape, shape),
        in_specs=[vmem, vmem],
        out_specs=(outside, outside),
        scratch_shapes=[pltpu.SemaphoreType.DMA((2, TILES))],
        compiler_params=pltpu.CompilerParams(vmem_limit_bytes=1 << 20),
        name="deliver",
    )(first, second)


def body(params, momentum, gradient, chosen_rows, live_counts, common_rows):
    high, low = table_parts()
    gather = np.concatenate([high.T, low.T, high.T], axis=1)
    gather = jnp.asarray(np.concatenate([gather, np.zeros_like(gather)], axis=0))
    inverse = jnp.asarray(np.concatenate([high, low, high], axis=1))
    new_params, residual = step(
        gather, inverse, common_rows[0].T, chosen_rows[0, 0].T, live_counts[0], momentum[0, 0], gradient[0, 0], params
    )
    new_params, residual = deliver(new_params, residual)
    return (new_params, residual[None, None])


def solution(mesh):
    placed = (
        P(),
        P("row", "col", None, None),
        P("row", "col", None, None),
        P("row", "col", None, None),
        P("row", "col", None),
        P("col", None, None),
    )
    return jax.shard_map(
        body,
        mesh=mesh,
        in_specs=placed,
        out_specs=(P(), P("row", "col", None, None)),
        check_vma=False,
    )
```

time: 59.7 us -> 40.8 us (0.68)
  Pallas kernels: 49.9 us -> 40 us
  local copies, waits for them, and re-layouts: 6.74 us -> 0 us
  other arithmetic: 1.99 us -> 0 us
    pallas_call x2, Pallas kernels: 49.9 us -> 40 us  [the longest x1 37.9 us: step(): pl.pallas_call(step_kernel, out_shape=(pltpu.VMEM((CH, W), f32), pltpu.VM...]
    unnamed x3 -> x0, local copies, waits for them, and re-layouts: 3.96 us -> none
    reshape x2 -> x0, local copies, waits for them, and re-layouts: 1.57 us -> none  [the longest x1 0.89 us: body(): names = jnp.repeat(common.T, 32, axis=1)]
    select_n x2 -> x0, other arithmetic: 1.29 us -> none  [the longest x1 0.69 us: body(): chosen = jnp.where(live, chosen, -1)]
    broadcast_in_dim x1 -> x0, local copies, waits for them, and re-layouts: 0.87 us -> none  [body(): names = jnp.repeat(common.T, 32, axis=1)]
    reduce_or x1 -> x0, other arithmetic: 0.69 us -> none  [body(): found = jnp.any(common[:, :, None] == chosen[:, None, :], axis=-1)]
where the time goes in v2:
time: 40.8 us; the launch traced here: 40.7 us
  Pallas kernels  40 us (98%)
  between operations  0.64 us (2%)
    pallas_call x1, Pallas kernels, step(): pl.pallas_call(step_kernel, out_shape=(pltpu.VMEM((CH, W), f32), pltpu.VM...  37.9 us
    pallas_call x1, Pallas kernels, deliver(): pl.pallas_call(deliver_kernel, out_shape=(shape, shape), in_specs=[vmem,...  2.13 us

profile of v2, /device:TPU:1, one launch (start us, length us, event | category | flops | bytes accessed | tf_op | source)
XLA Modules:
  0.0 40.7 jit_solution(15715612262987011838)
XLA Ops:
  0.6 37.9 %step.1 = (f32[64,8192]{1,0:T(8,128)S(1)}, f32[64,8192]{1,0:T(8,128)S(1)}) custom-call(bf16[128,192]{1,0:T(8,128)(2,1)} %constant.4.clone.gather_hbm, bf16[64,192]{1,0:T(8,128)(2,1)} %constant.5.clone.inverse_hbm, s32[8,128]{1,0:T(8,128)} %bitcast.12, s32[4,128]{1,0:T(4,128)} %bitcast.13, s32[1,128]{1,0:T(1,128)} %bitcast.14, f32[64,8192]{1,0:T(8,128)} %bitcast.10, ...), custom_call_target="tpu_custom_call" | custom-call | tf_op jit(solution)/shard_map/step/pallas_call | solution.py:329
  38.5 2.1 %deliver.1 = (f32[64,8192]{1,0:T(8,128)}, f32[64,8192]{1,0:T(8,128)}) custom-call(f32[64,8192]{1,0:T(8,128)S(1)} %get-tuple-element.6.first_ref, f32[64,8192]{1,0:T(8,128)S(1)} %get-tuple-element.7.second_ref), custom_call_target="tpu_custom_call" | custom-call | tf_op jit(solution)/shard_map/deliver/pallas_call | solution.py:377

commit v3 on v2

--- a/solution.py
+++ b/solution.py
@@ -19,6 +19,8 @@
 TILE = 1024
 TILES = W // TILE
 SUB = 256
+GATHER_COPIES = 2 * (2 * 3 + 2 * 12 + 2 * 16)
+EARLY, LATE = (0, 1, 2), (3, 6, 4, 5, 7)
 VMEM_GRANT = 67043328 - 2 * 4 * CH * W - 4096
 
 decay_rate = 0.9
@@ -41,6 +43,11 @@
     return high, (back - high.astype(np.float32)).astype(bf16)
 
 
+def steps_by_distance():
+    steps = [(dy, dk, dx) for dy in range(NY) for dk in range(NCORE) for dx in range(NX)][1:]
+    return sorted(steps, key=lambda s: -(min(s[0], NY - s[0]) + min(s[2], NX - s[2])))
+
+
 def two_parts(value):
     high = value.astype(bf16)
     return high, (value - high.astype(f32)).astype(bf16)
@@ -50,9 +57,9 @@
     gather_hbm, inverse_hbm, common_hbm, chosen_hbm, counts_hbm, moment_ref, grad_ref, params_ref,
     out_ref, residual_ref,
     gather_ref, inverse_ref, common_ref, chosen_ref, counts_ref, small_sem,
-    decayed, grads, hot_wanted, hot_chosen, wanted_rows, chosen_rows, chosen_values, own, parts, values, names, mine,
+    decayed, grads, hot_wanted, hot_chosen, wanted_rows, chosen_rows, chosen_values, own, parts, values, near, names, mine,
     moment_sem, grad_sem, param_sem, name_send, name_recv, row_send, row_recv, deep_send, deep_recv,
-    first_send, first_recv, second_send, second_recv, pair_send, pair_recv,
+    gather_send, first_recv, second_recv, pair_recv,
 ):
     r = lax.axis_index("row")
     c = lax.axis_index("col")
@@ -63,6 +70,10 @@
     def in_plane(index):
         return (index // NX, z * NX + lax.rem(index, NX))
 
+    def shifted(dy, dk, dx):
+        row = lax.rem(y + dy, NY) * NCORE + lax.rem(core + dk, NCORE)
+        return row * NX + lax.rem(x + dx, NX)
+
     def along_x(d):
         return (r, z * NX + lax.rem(x + d, NX))
 
@@ -76,7 +87,7 @@
         return pl.ds(pl.multiple_of(index * size, size), size)
 
     def half_lanes(index, h):
-        return pl.ds(pl.multiple_of(index * OWN + 128 * h, 128), 128)
+        return pl.ds(pl.multiple_of(h * (W // 2) + 128 * index, 128), 128)
 
     def remote(src, dst, send, recv, device):
         return pltpu.make_async_remote_copy(
@@ -89,6 +100,17 @@
     def grad_in(t):
         return pltpu.make_async_copy(grad_ref.at[:, lanes(t, TILE)], grads.at[:, lanes(t, TILE)], grad_sem.at[t])
 
+    barrier = pltpu.get_barrier_semaphore()
+
+    def greet_deep(d, carry):
+        pl.semaphore_signal(barrier, inc=1, device_id=along_z(d), device_id_type=MESH)
+        return carry
+
+    for step in steps_by_distance():
+        there = shifted(*step)
+        pl.semaphore_signal(barrier, inc=1, device_id=in_plane(there), device_id_type=MESH)
+
+    lax.fori_loop(1, NZ, greet_deep, 0)
     smalls = [
         pltpu.make_async_copy(src, dst, small_sem.at[i])
         for i, (src, dst) in enumerate(
@@ -103,24 +125,14 @@
     ]
     for copy in smalls:
         copy.start()
-    for t in range(TILES):
+    for t in range(TILES // 2):
         moment_in(t).start()
         grad_in(t).start()
-    params_in = pltpu.make_async_copy(params_ref.at[:, lanes(m, OWN)], mine, param_sem)
-    params_in.start()
-    barrier = pltpu.get_barrier_semaphore()
-
-    def greet_plane(d, carry):
-        pl.semaphore_signal(barrier, inc=1, device_id=in_plane(lax.rem(m + d, PLANE)), device_id_type=MESH)
-        return carry
-
-    def greet_deep(d, carry):
-        pl.semaphore_signal(barrier, inc=1, device_id=along_z(d), device_id_type=MESH)
-        return carry
-
-    lax.fori_loop(1, NZ, greet_deep, 0)
-    lax.fori_loop(1, PLANE, greet_plane, 0)
-
+    params_in = [
+        pltpu.make_async_copy(params_ref.at[:, half_lanes(m, h)], mine.at[h], param_sem.at[h]) for h in range(2)
+    ]
+    for copy in params_in:
+        copy.start()
     for copy in smalls:
         copy.wait()
     common = common_ref[...]
@@ -139,12 +151,18 @@
         hot_wanted[...].astype(bf16), gather_ref[...], preferred_element_type=f32
     ).astype(bf16)
     chosen_rows[...] = jnp.dot(hot_chosen[...].astype(bf16), gather_ref[...], preferred_element_type=f32)
-    names[z, x] = common
+    near[x] = common.astype(f32)
     left_lane = lax.broadcasted_iota(jnp.int32, (8, 128), 1) < CH
 
     def local_sums(t, carry):
         moment_in(t).wait()
         grad_in(t).wait()
+
+        @pl.when(t < TILES // 2)
+        def _():
+            moment_in(t + TILES // 2).start()
+            grad_in(t + TILES // 2).start()
+
         for i in range(TILE // SUB):
             at = pl.ds(pl.multiple_of(t * TILE + i * SUB, SUB), SUB)
             field = decay_rate * decayed[:, at] + grads[:, at]
@@ -167,25 +185,30 @@
             chosen_values[:, at] = picked[4 * Q :]
         return carry
 
-    lax.fori_loop(0, TILES, local_sums, 0)
-    pl.semaphore_wait(barrier, PLANE - 1 + NZ - 1)
-
-    for d in range(1, NX):
-        remote(common_ref, names.at[z, x], name_send.at[0], name_recv.at[0], along_x(d)).start()
-    for h in range(2):
-
-        def send_part(d, carry):
-            there = lax.rem(m + d, PLANE)
+    for h in range(2):
+        lax.fori_loop(h * (TILES // 2), (h + 1) * (TILES // 2), local_sums, 0)
+        if h == 0:
+            pl.semaphore_wait(barrier, PLANE - 1 + NZ - 1)
+            for d in range(1, NX):
+                remote(near.at[x], near.at[x], name_send.at[0], name_recv.at[0], along_x(d)).start()
+
+        for step in steps_by_distance():
+            there = shifted(*step)
             remote(
                 own.at[:, half_lanes(there, h)], parts.at[h, m], row_send.at[h], row_recv.at[h], in_plane(there)
             ).start()
-            return carry
-
-        lax.fori_loop(1, PLANE, send_part, 0)
         parts[h, m] = own[:, half_lanes(m, h)]
-    some = names.at[0, pl.ds(0, NX - 1)]
+    some = near.at[pl.ds(0, NX - 1)]
     near_names = remote(some, some, name_send.at[0], name_recv.at[0], along_x(1))
     near_names.wait_recv()
+    lane = lax.broadcasted_iota(jnp.int32, (128, 128), 1)
+    block = lax.broadcasted_iota(jnp.int32, (128, 128), 0)
+    mine_of = m * 2 + lax.rem(lane, 2) + (SPANS // 2) * lax.rem(lane // 2, 2)
+    listed = jnp.zeros((Q, 128), f32)
+    for group in range(NX):
+        pick = jnp.where((block == mine_of) & (lane // 4 == group), 1.0, 0.0).astype(bf16)
+        listed = listed + jnp.dot(near[group].astype(bf16), pick, preferred_element_type=f32)
+    names[z] = listed
 
     def send_names(d, carry):
         remote(names.at[z], names.at[z], name_send.at[1], name_recv.at[1], along_z(d)).start()
@@ -208,6 +231,13 @@
 
     lax.fori_loop(0, TILES, residuals, 0)
 
+    def send_values(h, deep):
+        @pl.when(z != deep)
+        def _():
+            remote(
+                values.at[h, z], values.at[h, z], deep_send.at[h], deep_recv.at[h], (r, deep * NX + x)
+            ).start()
+
     rows_moved = []
     for h in range(2):
         some = parts.at[h, pl.ds(0, PLANE - 1)]
@@ -219,34 +249,32 @@
             for other in range(1, NY * NCORE):
                 total = total + parts[h, other * NX + group]
             values[h, z, group] = total
-
-        def send_values(d, carry):
-            remote(values.at[h, z], values.at[h, z], deep_send.at[h], deep_recv.at[h], along_z(d)).start()
-            return carry
-
-        lax.fori_loop(1, NZ, send_values, 0)
+        for deep in EARLY:
+            send_values(h, deep)
+    for h in range(2):
+        for deep in LATE:
+            send_values(h, deep)
 
     some = names.at[pl.ds(0, NZ - 1)]
     far_names = remote(some, some, name_send.at[1], name_recv.at[1], along_z(1))
     far_names.wait_recv()
-    listed = names[...].reshape(NZ * NX * Q, SPANS).astype(f32).astype(bf16)
-    lane = lax.broadcasted_iota(jnp.int32, (128, 128), 1)
-    block = lax.broadcasted_iota(jnp.int32, (128, 128), 0)
-    wide_lane = lax.broadcasted_iota(jnp.int32, (NZ * NX * Q, 128), 1)
-    wide_freq = lax.rem(wide_lane, CH).astype(f32)
+    listed = names[...].reshape(NZ * Q, 128).astype(bf16)
+    wide_freq = lax.rem(lax.broadcasted_iota(jnp.int32, (NZ * NX * Q, 128), 1), CH).astype(f32)
     spreads = []
     for h in range(2):
-        pick = jnp.where(block == m * 4 + 2 * h + lane // CH, 1.0, 0.0).astype(bf16)
-        spread_names = jnp.dot(listed, pick, preferred_element_type=f32)
-        spreads.append(jnp.where(spread_names == wide_freq, 1.0, 0.0).T.astype(bf16))
-    params_in.wait()
+        found_names = []
+        for group in range(NX):
+            pick = jnp.where(block == 4 * group + 2 * h + lane // CH, 1.0, 0.0).astype(bf16)
+            found_names.append(jnp.dot(listed, pick, preferred_element_type=f32).reshape(NZ, Q, 128))
+        spread_names = jnp.stack(found_names, axis=1).reshape(NZ * NX * Q, 128)
+        hot = jnp.where(spread_names == wide_freq, 1.0, 0.0).T.astype(bf16)
+        spreads.append(jnp.dot(inverse_ref[...], hot, preferred_element_type=f32).astype(bf16))
+    for copy in params_in:
+        copy.wait()
     left = lax.broadcasted_iota(jnp.int32, (CH, 128), 1) < CH
-
-    started = []
 
     def go(copy):
         copy.start()
-        started.append(copy)
         return copy
 
     def place_of(h, rows, index):
@@ -254,15 +282,13 @@
 
     def send(h, rows, index, sems, slot, device):
         at = place_of(h, rows, index)
-        return go(remote(at, at, sems[0].at[h, slot], sems[1].at[h, slot], device))
-
-    first = (first_send, first_recv)
-    second = (second_send, second_recv)
+        return go(remote(at, at, gather_send, sems.at[h, slot], device))
+
     partner = (y * NCORE + (1 - core), c)
 
     def to_partner(h, rows, index):
         at = place_of(h, rows, index)
-        go(remote(at, at, pair_send, pair_recv, partner))
+        go(remote(at, at, gather_send, pair_recv, partner))
 
     def at_x(d):
         return r * NX + lax.rem(x + NX - d, NX)
@@ -282,18 +308,17 @@
         deep_moved.append(moved)
         high, low = two_parts(values[h].reshape(NZ * NX * Q, 128))
         both = jnp.dot(spreads[h], high, preferred_element_type=f32)
-        both = both + jnp.dot(spreads[h], low, preferred_element_type=f32)
-        high, low = two_parts(jnp.where(left, both[:CH], both[CH:]))
-        update = jnp.dot(inverse_ref[...], jnp.concatenate([high, high, low], axis=0), preferred_element_type=f32)
-        out_ref[:, half_lanes(m, h)] = mine[:, 128 * h : 128 * h + 128] - step_size * update
-        one = [send(h, 0, m, first, d - 1, along_x(d)) for d in range(1, NX)]
-        two = [send(h, 1, m, first, 2 + d, along_y(d)) for d in range(1, NY)]
+        both = both[:128] + both[128:] + jnp.dot(spreads[h][:128], low, preferred_element_type=f32)
+        update = jnp.where(left, both[:CH], both[CH:])
+        out_ref[:, half_lanes(m, h)] = mine[h] - step_size * update
+        one = [send(h, 0, m, first_recv, d - 1, along_x(d)) for d in range(1, NX)]
+        two = [send(h, 1, m, first_recv, 2 + d, along_y(d)) for d in range(1, NY)]
         over_y = [[None] * NX for _ in range(NY)]
         over_x = [[None] * NY for _ in range(NX)]
         for d in range(1, NY):
-            over_y[d][0] = send(h, 0, m, second, (d - 1) * NX, along_y(d))
+            over_y[d][0] = send(h, 0, m, second_recv, (d - 1) * NX, along_y(d))
         for d in range(1, NX):
-            over_x[d][0] = send(h, 1, m, second, 12 + (d - 1) * NY, along_x(d))
+            over_x[d][0] = send(h, 1, m, second_recv, 12 + (d - 1) * NY, along_x(d))
         to_partner(h, 0, m)
         to_partner(h, 1, m)
         over.append((one, two, over_y, over_x))
@@ -302,11 +327,11 @@
         for j in range(1, 4):
             one[j - 1].wait_recv()
             for d in range(1, NY):
-                over_y[d][j] = send(h, 0, at_x(j), second, (d - 1) * NX + j, along_y(d))
+                over_y[d][j] = send(h, 0, at_x(j), second_recv, (d - 1) * NX + j, along_y(d))
             to_partner(h, 0, at_x(j))
             two[j - 1].wait_recv()
             for d in range(1, NX):
-                over_x[d][j] = send(h, 1, at_y(j), second, 12 + (d - 1) * NY + j, along_x(d))
+                over_x[d][j] = send(h, 1, at_y(j), second_recv, 12 + (d - 1) * NY + j, along_x(d))
             to_partner(h, 1, at_y(j))
     for h in range(2):
         one, two, over_y, over_x = over[h]
@@ -317,8 +342,10 @@
                 over_x[d][j].wait_recv()
                 to_partner(h, 1, at_both(j, d))
     some = out_ref.at[:, pl.ds(0, W // 2)]
-    remote(some, some, pair_send, pair_recv, partner).wait_recv()
-    for copy in started + rows_moved + deep_moved + [near_names, far_names]:
+    remote(some, some, gather_send, pair_recv, partner).wait_recv()
+    some = out_ref.at[:, pl.ds(0, GATHER_COPIES * 64)]
+    remote(some, some, gather_send, pair_recv, partner).wait_send()
+    for copy in rows_moved + deep_moved + [near_names, far_names]:
         copy.wait_send()
 
 
@@ -333,7 +360,7 @@
         out_specs=(vmem, vmem),
         scratch_shapes=[
             pltpu.VMEM((128, 3 * CH), bf16),
-            pltpu.VMEM((CH, 3 * CH), bf16),
+            pltpu.VMEM((256, 128), bf16),
             pltpu.VMEM((Q, SPANS), jnp.int32),
             pltpu.VMEM((S, SPANS), jnp.int32),
             pltpu.VMEM((1, SPANS), jnp.int32),
@@ -348,10 +375,11 @@
             pltpu.VMEM((Q, W), f32),
             pltpu.VMEM((2, PLANE, Q, 128), f32),
             pltpu.VMEM((2, NZ, NX, Q, 128), f32),
-            pltpu.VMEM((NZ, NX, Q, SPANS), jnp.int32),
-            pltpu.VMEM((CH, OWN), f32),
-            dma((TILES,)), dma((TILES,)), dma, dma((2,)), dma((2,)), dma((2,)), dma((2,)), dma((2,)), dma((2,)),
-            dma((2, 6)), dma((2, 6)), dma((2, 24)), dma((2, 24)), dma, dma,
+            pltpu.VMEM((NX, Q, SPANS), f32),
+            pltpu.VMEM((NZ, Q, 128), f32),
+            pltpu.VMEM((2, CH, 128), f32),
+            dma((TILES,)), dma((TILES,)), dma((2,)), dma((2,)), dma((2,)), dma((2,)), dma((2,)), dma((2,)), dma((2,)),
+            dma, dma((2, 6)), dma((2, 24)), dma,
         ],
         compiler_params=pltpu.CompilerParams(collective_id=0, has_side_effects=True, vmem_limit_bytes=VMEM_GRANT),
         name="step",
@@ -389,7 +417,7 @@
     high, low = table_parts()
     gather = np.concatenate([high.T, low.T, high.T], axis=1)
     gather = jnp.asarray(np.concatenate([gather, np.zeros_like(gather)], axis=0))
-    inverse = jnp.asarray(np.concatenate([high, low, high], axis=1))
+    inverse = jnp.asarray(np.concatenate([np.kron(np.eye(2, dtype=bf16), part) for part in (high, low)], axis=0))
     new_params, residual = step(
         gather, inverse, common_rows[0].T, chosen_rows[0, 0].T, live_counts[0], momentum[0, 0], gradient[0, 0], params
     )

time: 40.8 us -> 37.8 us (0.926)
  Pallas kernels: 40 us -> 37 us
    pallas_call x1, Pallas kernels: 37.9 us -> 34.9 us  [step(): pl.pallas_call(step_kernel, out_shape=(pltpu.VMEM((CH, W), f32), pltpu.VM...]
where the time goes in v3:
time: 37.8 us; the launch traced here: 37.7 us
  Pallas kernels  37 us (98%)
  between operations  0.64 us (2%)
    pallas_call x1, Pallas kernels, step(): pl.pallas_call(step_kernel, out_shape=(pltpu.VMEM((CH, W), f32), pltpu.VM...  34.9 us
    pallas_call x1, Pallas kernels, deliver(): pl.pallas_call(deliver_kernel, out_shape=(shape, shape), in_specs=[vmem,...  2.13 us

profile of v3, /device:TPU:1, one launch (start us, length us, event | category | flops | bytes accessed | tf_op | source)
XLA Modules:
  0.0 37.7 jit_solution(12563940026485600749)
XLA Ops:
  0.6 34.9 %step.1 = (f32[64,8192]{1,0:T(8,128)S(1)}, f32[64,8192]{1,0:T(8,128)S(1)}) custom-call(bf16[128,192]{1,0:T(8,128)(2,1)} %constant.4.clone.gather_hbm, bf16[256,128]{1,0:T(8,128)(2,1)} %constant.5.clone.inverse_hbm, s32[8,128]{1,0:T(8,128)} %bitcast.12, s32[4,128]{1,0:T(4,128)} %bitcast.13, s32[1,128]{1,0:T(1,128)} %bitcast.14, f32[64,8192]{1,0:T(8,128)} %bitcast.10, ...), custom_call_target="tpu_custom_call" | custom-call | tf_op jit(solution)/shard_map/step/pallas_call | solution.py:356
  35.5 2.1 %deliver.1 = (f32[64,8192]{1,0:T(8,128)}, f32[64,8192]{1,0:T(8,128)}) custom-call(f32[64,8192]{1,0:T(8,128)S(1)} %get-tuple-element.6.first_ref, f32[64,8192]{1,0:T(8,128)S(1)} %get-tuple-element.7.second_ref), custom_call_target="tpu_custom_call" | custom-call | tf_op jit(solution)/shard_map/deliver/pallas_call | solution.py:405

commit v4 on v3

--- a/solution.py
+++ b/solution.py
@@ -311,32 +311,34 @@
         both = both[:128] + both[128:] + jnp.dot(spreads[h][:128], low, preferred_element_type=f32)
         update = jnp.where(left, both[:CH], both[CH:])
         out_ref[:, half_lanes(m, h)] = mine[h] - step_size * update
-        one = [send(h, 0, m, first_recv, d - 1, along_x(d)) for d in range(1, NX)]
-        two = [send(h, 1, m, first_recv, 2 + d, along_y(d)) for d in range(1, NY)]
+        one, two = [None] * 3, [None] * 3
+        for d in (2, 1, 3):
+            one[d - 1] = send(h, 0, m, first_recv, d - 1, along_x(d))
+            two[d - 1] = send(h, 1, m, first_recv, 2 + d, along_y(d))
         over_y = [[None] * NX for _ in range(NY)]
         over_x = [[None] * NY for _ in range(NX)]
-        for d in range(1, NY):
+        for d in (2, 1, 3):
             over_y[d][0] = send(h, 0, m, second_recv, (d - 1) * NX, along_y(d))
-        for d in range(1, NX):
+        for d in (2, 1, 3):
             over_x[d][0] = send(h, 1, m, second_recv, 12 + (d - 1) * NY, along_x(d))
         to_partner(h, 0, m)
         to_partner(h, 1, m)
         over.append((one, two, over_y, over_x))
     for h in range(2):
         one, two, over_y, over_x = over[h]
-        for j in range(1, 4):
+        for j in (1, 3, 2):
             one[j - 1].wait_recv()
-            for d in range(1, NY):
+            for d in (2, 1, 3):
                 over_y[d][j] = send(h, 0, at_x(j), second_recv, (d - 1) * NX + j, along_y(d))
             to_partner(h, 0, at_x(j))
             two[j - 1].wait_recv()
-            for d in range(1, NX):
+            for d in (2, 1, 3):
                 over_x[d][j] = send(h, 1, at_y(j), second_recv, 12 + (d - 1) * NY + j, along_x(d))
             to_partner(h, 1, at_y(j))
     for h in range(2):
         one, two, over_y, over_x = over[h]
-        for j in range(4):
-            for d in range(1, 4):
+        for j in (0, 1, 3, 2):
+            for d in (1, 3, 2):
                 over_y[d][j].wait_recv()
                 to_partner(h, 0, at_both(d, j))
                 over_x[d][j].wait_recv()

time: 37.8 us -> 37.6 us (level)
  no operation moved by 1% of the time
where the time goes in v4:
time: 37.6 us; the launch traced here: 37.5 us
  Pallas kernels  36.8 us (98%)
  between operations  0.64 us (2%)
    pallas_call x1, Pallas kernels, step(): pl.pallas_call(step_kernel, out_shape=(pltpu.VMEM((CH, W), f32), pltpu.VM...  34.7 us
    pallas_call x1, Pallas kernels, deliver(): pl.pallas_call(deliver_kernel, out_shape=(shape, shape), in_specs=[vmem,...  2.13 us

profile of v4, /device:TPU:1, one launch (start us, length us, event | category | flops | bytes accessed | tf_op | source)
XLA Modules:
  0.0 37.5 jit_solution(15830393763158884617)
XLA Ops:
  0.6 34.7 %step.1 = (f32[64,8192]{1,0:T(8,128)S(1)}, f32[64,8192]{1,0:T(8,128)S(1)}) custom-call(bf16[128,192]{1,0:T(8,128)(2,1)} %constant.4.clone.gather_hbm, bf16[256,128]{1,0:T(8,128)(2,1)} %constant.5.clone.inverse_hbm, s32[8,128]{1,0:T(8,128)} %bitcast.12, s32[4,128]{1,0:T(4,128)} %bitcast.13, s32[1,128]{1,0:T(1,128)} %bitcast.14, f32[64,8192]{1,0:T(8,128)} %bitcast.10, ...), custom_call_target="tpu_custom_call" | custom-call | tf_op jit(solution)/shard_map/step/pallas_call | solution.py:358
  35.3 2.1 %deliver.1 = (f32[64,8192]{1,0:T(8,128)}, f32[64,8192]{1,0:T(8,128)}) custom-call(f32[64,8192]{1,0:T(8,128)S(1)} %get-tuple-element.6.first_ref, f32[64,8192]{1,0:T(8,128)S(1)} %get-tuple-element.7.second_ref), custom_call_target="tpu_custom_call" | custom-call | tf_op jit(solution)/shard_map/deliver/pallas_call | solution.py:407

commit v5 on v4

--- a/solution.py
+++ b/solution.py
@@ -19,6 +19,7 @@
 TILE = 1024
 TILES = W // TILE
 SUB = 256
+FIRST = (0, 1, 3, 2)
 GATHER_COPIES = 2 * (2 * 3 + 2 * 12 + 2 * 16)
 EARLY, LATE = (0, 1, 2), (3, 6, 4, 5, 7)
 VMEM_GRANT = 67043328 - 2 * 4 * CH * W - 4096
@@ -280,9 +281,27 @@
     def place_of(h, rows, index):
         return out_ref.at[pl.ds(32 * rows, 32), half_lanes(index, h)]
 
-    def send(h, rows, index, sems, slot, device):
+    def send(h, rows, index, sem, device):
         at = place_of(h, rows, index)
-        return go(remote(at, at, gather_send, sems.at[h, slot], device))
+        go(remote(at, at, gather_send, sem, device))
+
+    def arrived(h, rows, index, sem):
+        at = place_of(h, rows, index)
+        remote(at, at, gather_send, sem, partner).wait_recv()
+
+    def send_over_x(h, rows, index, sem_of):
+        for there in FIRST:
+
+            @pl.when(x != there)
+            def _():
+                send(h, rows, index, sem_of(lax.rem(there + NX - x, NX)), (r, z * NX + there))
+
+    def send_over_y(h, rows, index, sem_of):
+        for there in FIRST:
+
+            @pl.when(y != there)
+            def _():
+                send(h, rows, index, sem_of(lax.rem(there + NY - y, NY)), (there * NCORE + core, c))
 
     partner = (y * NCORE + (1 - core), c)
 
@@ -300,7 +319,6 @@
         return (lax.rem(y + NY - dy, NY) * NCORE + core) * NX + lax.rem(x + NX - dx, NX)
 
     deep_moved = []
-    over = []
     for h in range(2):
         some = values.at[h, pl.ds(0, NZ - 1)]
         moved = remote(some, some, deep_send.at[h], deep_recv.at[h], along_z(1))
@@ -311,37 +329,26 @@
         both = both[:128] + both[128:] + jnp.dot(spreads[h][:128], low, preferred_element_type=f32)
         update = jnp.where(left, both[:CH], both[CH:])
         out_ref[:, half_lanes(m, h)] = mine[h] - step_size * update
-        one, two = [None] * 3, [None] * 3
-        for d in (2, 1, 3):
-            one[d - 1] = send(h, 0, m, first_recv, d - 1, along_x(d))
-            two[d - 1] = send(h, 1, m, first_recv, 2 + d, along_y(d))
-        over_y = [[None] * NX for _ in range(NY)]
-        over_x = [[None] * NY for _ in range(NX)]
-        for d in (2, 1, 3):
-            over_y[d][0] = send(h, 0, m, second_recv, (d - 1) * NX, along_y(d))
-        for d in (2, 1, 3):
-            over_x[d][0] = send(h, 1, m, second_recv, 12 + (d - 1) * NY, along_x(d))
+        send_over_x(h, 0, m, lambda d: first_recv.at[h, d - 1])
+        send_over_y(h, 1, m, lambda d: first_recv.at[h, 2 + d])
+        send_over_y(h, 0, m, lambda d: second_recv.at[h, (d - 1) * NX])
+        send_over_x(h, 1, m, lambda d: second_recv.at[h, 12 + (d - 1) * NY])
         to_partner(h, 0, m)
         to_partner(h, 1, m)
-        over.append((one, two, over_y, over_x))
-    for h in range(2):
-        one, two, over_y, over_x = over[h]
+    for h in range(2):
         for j in (1, 3, 2):
-            one[j - 1].wait_recv()
-            for d in (2, 1, 3):
-                over_y[d][j] = send(h, 0, at_x(j), second_recv, (d - 1) * NX + j, along_y(d))
+            arrived(h, 0, at_x(j), first_recv.at[h, j - 1])
+            send_over_y(h, 0, at_x(j), lambda d: second_recv.at[h, (d - 1) * NX + j])
             to_partner(h, 0, at_x(j))
-            two[j - 1].wait_recv()
-            for d in (2, 1, 3):
-                over_x[d][j] = send(h, 1, at_y(j), second_recv, 12 + (d - 1) * NY + j, along_x(d))
+            arrived(h, 1, at_y(j), first_recv.at[h, 2 + j])
+            send_over_x(h, 1, at_y(j), lambda d: second_recv.at[h, 12 + (d - 1) * NY + j])
             to_partner(h, 1, at_y(j))
     for h in range(2):
-        one, two, over_y, over_x = over[h]
         for j in (0, 1, 3, 2):
             for d in (1, 3, 2):
-                over_y[d][j].wait_recv()
+                arrived(h, 0, at_both(d, j), second_recv.at[h, (d - 1) * NX + j])
                 to_partner(h, 0, at_both(d, j))
-                over_x[d][j].wait_recv()
+                arrived(h, 1, at_both(j, d), second_recv.at[h, 12 + (d - 1) * NY + j])
                 to_partner(h, 1, at_both(j, d))
     some = out_ref.at[:, pl.ds(0, W // 2)]
     remote(some, some, gather_send, pair_recv, partner).wait_recv()

time: 37.6 us -> 37.6 us (level)
  no operation moved by 1% of the time
where the time goes in v5:
time: 37.6 us; the launch traced here: 37.5 us
  Pallas kernels  36.9 us (98%)
  between operations  0.64 us (2%)
    pallas_call x1, Pallas kernels, step(): pl.pallas_call(step_kernel, out_shape=(pltpu.VMEM((CH, W), f32), pltpu.VM...  34.7 us
    pallas_call x1, Pallas kernels, deliver(): pl.pallas_call(deliver_kernel, out_shape=(shape, shape), in_specs=[vmem,...  2.13 us

profile of v5, /device:TPU:1, one launch (start us, length us, event | category | flops | bytes accessed | tf_op | source)
XLA Modules:
  0.0 37.5 jit_solution(8379274347819715452)
XLA Ops:
  0.6 34.7 %step.1 = (f32[64,8192]{1,0:T(8,128)S(1)}, f32[64,8192]{1,0:T(8,128)S(1)}) custom-call(bf16[128,192]{1,0:T(8,128)(2,1)} %constant.4.clone.gather_hbm, bf16[256,128]{1,0:T(8,128)(2,1)} %constant.5.clone.inverse_hbm, s32[8,128]{1,0:T(8,128)} %bitcast.12, s32[4,128]{1,0:T(4,128)} %bitcast.13, s32[1,128]{1,0:T(1,128)} %bitcast.14, f32[64,8192]{1,0:T(8,128)} %bitcast.10, ...), custom_call_target="tpu_custom_call" | custom-call | tf_op jit(solution)/shard_map/step/pallas_call | solution.py:365
  35.4 2.1 %deliver.1 = (f32[64,8192]{1,0:T(8,128)}, f32[64,8192]{1,0:T(8,128)}) custom-call(f32[64,8192]{1,0:T(8,128)S(1)} %get-tuple-element.6.first_ref, f32[64,8192]{1,0:T(8,128)S(1)} %get-tuple-element.7.second_ref), custom_call_target="tpu_custom_call" | custom-call | tf_op jit(solution)/shard_map/deliver/pallas_call | solution.py:414
